TPU v7x, 512 devices: a whole 4x8x8 slice. The times are simulated.
512 devices in a mesh: row: 16 (over z, core), col: 32 (over y, x).
Axes of the slice: x: 4, y: 8, z: 8, core: 2. Of those that a mesh axis runs over, the one named last changes fastest.
Arguments:
- embeddings: bfloat16 [2048, 512], P('row'), may hold values from -6 to 6
- row_weight: bfloat16 [512, 32], replicated, may hold values from -0.25 to 0.25
- col_weight: bfloat16 [512, 32], replicated, may hold values from -0.25 to 0.25
- conv_weights: bfloat16 [3, 32, 32, 3, 3], replicated, may hold values from -0.5 to 0.5
- conv_bias: float32 [3, 32], replicated, may hold values from -3 to 3
- head_weight: bfloat16 [32], replicated, may hold values from -1 to 1
Outputs:
- contact_map: float32 [2048, 2048], P('row', 'col')
All inputs are finite; a program needn't handle non-finite values.
Results may differ from a plain program's by a relative error of at most 0.023.
Values may be sent and summed in bfloat16 or wider, within the bound.
A program may use at most 64 MiB of HBM per device.

v0:
```python
import jax
import jax.numpy as jnp
from jax import lax
from jax.sharding import PartitionSpec as P


def spread(value, axis, source):
    kept = jnp.where(lax.axis_index(axis) == source, value, 0).astype(value.dtype)
    return lax.psum(kept, axis)


def extended(cells, sides, width):
    for axis, dim in sides:
        count = lax.axis_size(axis)
        ends = count - 1
        head = lax.slice_in_dim(cells, 0, width, axis=dim)
        tail = lax.slice_in_dim(cells, cells.shape[dim] - width, cells.shape[dim], axis=dim)
        cells = jnp.concatenate(
            [
                lax.ppermute(tail, axis, [(i, (i + 1) % count) for i in range(ends)]),
                cells,
                lax.ppermute(head, axis, [((i + 1) % count, i) for i in range(ends)]),
            ],
            axis=dim,
        )
    return cells


def dilated_level(padded, weight, level_bias, dilation):
    summed = lax.conv_general_dilated(
        padded[None],
        weight,
        (1, 1),
        "VALID",
        rhs_dilation=(dilation, dilation),
        dimension_numbers=("NCHW", "OIHW", "NCHW"),
        preferred_element_type=jnp.float32,
    )[0]
    return jax.nn.relu(summed + level_bias[:, None, None]).astype(jnp.bfloat16)


def pair_tile(rows_part, cols_part):
    return (
        rows_part.T.astype(jnp.float32)[:, :, None] + cols_part.T.astype(jnp.float32)[:, None, :]
    ).astype(jnp.bfloat16)


def body(embeddings, row_weight, col_weight, conv_weights, conv_bias, head_weight):
    row_bins = embeddings.shape[0]
    total_bins = row_bins * lax.axis_size("row")
    col_bins = total_bins // lax.axis_size("col")
    first_col = lax.axis_index("col") * col_bins
    owner_row = first_col // row_bins
    offset = first_col - owner_row * row_bins
    dilations = (1, 2, 4)
    row_feats = jnp.dot(embeddings, row_weight, preferred_element_type=jnp.float32).astype(
        jnp.bfloat16
    )
    owner_block = spread(embeddings, "row", owner_row)
    col_rows = lax.dynamic_slice_in_dim(owner_block, offset, col_bins, 0)
    col_feats = jnp.dot(col_rows, col_weight, preferred_element_type=jnp.float32).astype(
        jnp.bfloat16
    )
    current = pair_tile(row_feats, col_feats)
    for level_number, dilation in enumerate(dilations):
        padded = extended(current, (("row", 1), ("col", 2)), dilation)
        current = dilated_level(
            padded, conv_weights[level_number], conv_bias[level_number], dilation
        )
    return jnp.einsum("c,crj->rj", head_weight, current, preferred_element_type=jnp.float32)


def solution(mesh):
    return jax.shard_map(
        body,
        mesh=mesh,
        in_specs=(P("row", None), P(), P(), P(), P(), P()),
        out_specs=P("row", "col"),
        check_vma=False,
    )
```

profile of v0, /device:TPU:223, one launch (start us, length us, event | category | flops | bytes accessed | tf_op | source)
XLA Modules:
  0.0 261.4 jit_solution(6402877888625267361)
XLA Ops:
  9.2 117.9 %all-reduce.2.cloned.1.call-done = bf16[128,512]{1,0:T(8,128)(2,1)} async-done(((bf16[128,512]{1,0:T(8,128)(2,1)}), bf16[128,512]{1,0:T(8,128)(2,1)}) %all-reduce.2.cloned.1.call-update) | async-done | bytes 131088 | tf_op jit(solution)/shard_map/psum | solution.py:9
  128.7 4.1 %collective-permute-start = (bf16[32,1,64]{1,0,2:T(8,128)(2,1)S(1)}, bf16[32,1,64]{1,0,2:T(8,128)(2,1)S(1)}, u32[]{:S(2)}, u32[]{:S(2)}) collective-permute-start(bf16[32,1,64]{1,0,2:T(8,128)(2,1)S(1)} %get-tuple-element.15), channel_id=1, source_target_pairs={{0,32},{32,64},{64,96},{96,128},{128,160},{160,192},{192,224},{224... | collective-permute-start | bytes 12296 | tf_op jit(solution)/shard_map/ppermute | solution.py:20
  132.8 1.9 collective-permute-start.1
  134.8 4.2 %collective-permute-done = bf16[32,1,64]{1,0,2:T(8,128)(2,1)S(1)} collective-permute-done((bf16[32,1,64]{1,0,2:T(8,128)(2,1)S(1)}, bf16[32,1,64]{1,0,2:T(8,128)(2,1)S(1)}, u32[]{:S(2)}, u32[]{:S(2)}) %collective-permute-start) | collective-permute-done | bytes 4128 | tf_op jit(solution)/shard_map/ppermute | solution.py:20
  138.9 5.6 %collective-permute-done.1 = bf16[32,1,64]{1,0,2:T(8,128)(2,1)S(1)} collective-permute-done((bf16[32,1,64]{1,0,2:T(8,128)(2,1)S(1)}, bf16[32,1,64]{1,0,2:T(8,128)(2,1)S(1)}, u32[]{:S(2)}, u32[]{:S(2)}) %collective-permute-start.1) | collective-permute-done | bytes 4128 | tf_op jit(solution)/shard_map/ppermute | solution.py:22
  144.6 4.3 %collective-permute-start.2 = (bf16[32,130,1]{1,0,2:T(8,128)(2,1)S(1)}, bf16[32,130,1]{1,0,2:T(8,128)(2,1)S(1)}, u32[]{:S(2)}, u32[]{:S(2)}) collective-permute-start(bf16[32,130,1]{1,0,2:T(8,128)(2,1)S(1)} %get-tuple-element.9), channel_id=1, source_target_pairs={{0,1},{1,2},{2,3},{3,4},{4,5},{5,6},{6,7},{7,8},{8,9},{9,10},{10,1... | collective-permute-start | bytes 24968 | tf_op jit(solution)/shard_map/ppermute | solution.py:20
  149.0 1.9 collective-permute-start.3
  150.9 5.8 %collective-permute-done.3 = bf16[32,130,1]{1,0,2:T(8,128)(2,1)S(1)} collective-permute-done((bf16[32,130,1]{1,0,2:T(8,128)(2,1)S(1)}, bf16[32,130,1]{1,0,2:T(8,128)(2,1)S(1)}, u32[]{:S(2)}, u32[]{:S(2)}) %collective-permute-start.3) | collective-permute-done | bytes 8352 | tf_op jit(solution)/shard_map/ppermute | solution.py:22
  157.8 3.1 %copy.32 = bf16[32,130,1,8,9]{0,3,4,1,2:T(8,128)(2,1)} copy(bf16[32,130,1,8,9]{1,0,4,3,2:T(8,128)(2,1)S(1)} %bitcast.84) | data formatting | bytes 1198080 | tf_op jit(solution)/shard_map/conv_general_dilated | solution.py:30
  162.1 6.6 %broadcast_select_fusion.2 = f32[128,8,9,32]{3,1,2,0:T(8,128)} fusion(pred[8,9]{0,1:T(8,128)(4,1)S(1)} %copy-done.4, bf16[32,130,1,7,2]{0,3,4,1,2:T(8,128)(2,1)S(1)} %slice.80, bf16[32,130,1,8,9]{0,3,4,1,2:T(8,128)(2,1)} %copy.32, bf16[3,32,32,3,3]{2,1,4,3,0:T(8,128)(2,1)S(1)} %copy-done.3), kind=kOutput, calls=%fused_computation.27 | convolution fusion | flops 172360704 | bytes 2386944 | tf_op jit(solution)/shard_map/conv_general_dilated | solution.py:30
  168.6 3.7 %copy.33 = f32[128,8,9,32]{0,3,2,1:T(8,128)S(1)} copy(f32[128,8,9,32]{3,1,2,0:T(8,128)} %broadcast_select_fusion.2) | data formatting | bytes 2359296 | tf_op jit(solution)/shard_map/conv_general_dilated | solution.py:30
  172.8 3.2 %collective-permute-start.4 = (bf16[32,2,64]{1,0,2:T(8,128)(2,1)S(1)}, bf16[32,2,64]{1,0,2:T(8,128)(2,1)S(1)}, u32[]{:S(2)}, u32[]{:S(2)}) collective-permute-start(bf16[32,2,64]{1,0,2:T(8,128)(2,1)S(1)} %get-tuple-element.13), channel_id=1, source_target_pairs={{0,32},{32,64},{64,96},{96,128},{128,160},{160,192},{192,224},{224... | collective-permute-start | bytes 24584 | tf_op jit(solution)/shard_map/ppermute | solution.py:20
  176.0 1.9 collective-permute-start.5
  177.9 4.2 %collective-permute-done.4 = bf16[32,2,64]{1,0,2:T(8,128)(2,1)S(1)} collective-permute-done((bf16[32,2,64]{1,0,2:T(8,128)(2,1)S(1)}, bf16[32,2,64]{1,0,2:T(8,128)(2,1)S(1)}, u32[]{:S(2)}, u32[]{:S(2)}) %collective-permute-start.4) | collective-permute-done | bytes 8224 | tf_op jit(solution)/shard_map/ppermute | solution.py:20
  182.1 5.6 %collective-permute-done.5 = bf16[32,2,64]{1,0,2:T(8,128)(2,1)S(1)} collective-permute-done((bf16[32,2,64]{1,0,2:T(8,128)(2,1)S(1)}, bf16[32,2,64]{1,0,2:T(8,128)(2,1)S(1)}, u32[]{:S(2)}, u32[]{:S(2)}) %collective-permute-start.5) | collective-permute-done | bytes 8224 | tf_op jit(solution)/shard_map/ppermute | solution.py:22
  187.8 1.9 collective-permute-start.6
  189.7 3.4 %collective-permute-start.7 = (bf16[32,132,2]{1,0,2:T(8,128)(2,1)S(1)}, bf16[32,132,2]{1,0,2:T(8,128)(2,1)S(1)}, u32[]{:S(2)}, u32[]{:S(2)}) collective-permute-start(bf16[32,132,2]{1,0,2:T(8,128)(2,1)S(1)} %get-tuple-element.8), channel_id=1, source_target_pairs={{1,0},{2,1},{3,2},{4,3},{5,4},{6,5},{7,6},{8,7},{9,8},{10,9},{11,1... | collective-permute-start | bytes 50696 | tf_op jit(solution)/shard_map/ppermute | solution.py:22
  193.1 4.6 %collective-permute-done.7 = bf16[32,132,2]{1,0,2:T(8,128)(2,1)S(1)} collective-permute-done((bf16[32,132,2]{1,0,2:T(8,128)(2,1)S(1)}, bf16[32,132,2]{1,0,2:T(8,128)(2,1)S(1)}, u32[]{:S(2)}, u32[]{:S(2)}) %collective-permute-start.7) | collective-permute-done | bytes 16928 | tf_op jit(solution)/shard_map/ppermute | solution.py:22
  199.6 3.3 %copy.35 = bf16[32,132,1,8,9]{0,3,4,1,2:T(8,128)(2,1)S(1)} copy(bf16[32,132,1,8,9]{1,0,4,3,2:T(8,128)(2,1)} %bitcast.82) | data formatting | bytes 1216512 | tf_op jit(solution)/shard_map/conv_general_dilated | solution.py:30
  203.2 5.5 %broadcast_select_fusion.1 = f32[128,8,9,32]{3,1,2,0:T(8,128)} fusion(pred[8,9]{0,1:T(8,128)(4,1)S(1)} %copy-done.4, bf16[32,132,1,7,4]{0,3,4,1,2:T(8,128)(2,1)S(1)} %slice.84, bf16[32,132,1,8,9]{0,3,4,1,2:T(8,128)(2,1)S(1)} %copy.35, bf16[3,32,32,3,3]{2,1,4,3,0:T(8,128)(2,1)S(1)} %copy-done.3), kind=kOutput, calls=%fused_computation.26 | convolution fusion | flops 172800000 | bytes 4769792 | tf_op jit(solution)/shard_map/conv_general_dilated | solution.py:30
  208.7 3.7 %copy.36 = f32[128,8,9,32]{0,3,2,1:T(8,128)S(1)} copy(f32[128,8,9,32]{3,1,2,0:T(8,128)} %broadcast_select_fusion.1) | data formatting | bytes 2359296 | tf_op jit(solution)/shard_map/conv_general_dilated | solution.py:30
  212.8 2.9 %collective-permute-start.8 = (bf16[32,4,64]{1,0,2:T(8,128)(2,1)S(1)}, bf16[32,4,64]{1,0,2:T(8,128)(2,1)S(1)}, u32[]{:S(2)}, u32[]{:S(2)}) collective-permute-start(bf16[32,4,64]{1,0,2:T(8,128)(2,1)S(1)} %get-tuple-element.11), channel_id=1, source_target_pairs={{0,32},{32,64},{64,96},{96,128},{128,160},{160,192},{192,224},{224... | collective-permute-start | bytes 49160 | tf_op jit(solution)/shard_map/ppermute | solution.py:20
  215.7 1.9 collective-permute-start.9
  217.7 4.2 %collective-permute-done.8 = bf16[32,4,64]{1,0,2:T(8,128)(2,1)S(1)} collective-permute-done((bf16[32,4,64]{1,0,2:T(8,128)(2,1)S(1)}, bf16[32,4,64]{1,0,2:T(8,128)(2,1)S(1)}, u32[]{:S(2)}, u32[]{:S(2)}) %collective-permute-start.8) | collective-permute-done | bytes 16416 | tf_op jit(solution)/shard_map/ppermute | solution.py:20
  221.9 5.6 %collective-permute-done.9 = bf16[32,4,64]{1,0,2:T(8,128)(2,1)S(1)} collective-permute-done((bf16[32,4,64]{1,0,2:T(8,128)(2,1)S(1)}, bf16[32,4,64]{1,0,2:T(8,128)(2,1)S(1)}, u32[]{:S(2)}, u32[]{:S(2)}) %collective-permute-start.9) | collective-permute-done | bytes 16416 | tf_op jit(solution)/shard_map/ppermute | solution.py:22
  227.6 1.9 collective-permute-start.10
  229.5 3.5 %collective-permute-start.11 = (bf16[32,136,4]{1,0,2:T(8,128)(2,1)S(1)}, bf16[32,136,4]{1,0,2:T(8,128)(2,1)S(1)}, u32[]{:S(2)}, u32[]{:S(2)}) collective-permute-start(bf16[32,136,4]{1,0,2:T(8,128)(2,1)S(1)} %get-tuple-element.6), channel_id=1, source_target_pairs={{1,0},{2,1},{3,2},{4,3},{5,4},{6,5},{7,6},{8,7},{9,8},{10,9},{11,1... | collective-permute-start | bytes 104456 | tf_op jit(solution)/shard_map/ppermute | solution.py:22
  233.1 4.8 %collective-permute-done.11 = bf16[32,136,4]{1,0,2:T(8,128)(2,1)S(1)} collective-permute-done((bf16[32,136,4]{1,0,2:T(8,128)(2,1)S(1)}, bf16[32,136,4]{1,0,2:T(8,128)(2,1)S(1)}, u32[]{:S(2)}, u32[]{:S(2)}) %collective-permute-start.11) | collective-permute-done | bytes 34848 | tf_op jit(solution)/shard_map/ppermute | solution.py:22
  237.8 1.6 pad_maximum_fusion
  239.5 3.0 %copy.38 = bf16[32,136,1,8,9]{0,3,4,1,2:T(8,128)(2,1)S(1)} copy(bf16[32,136,1,8,9]{1,0,4,3,2:T(8,128)(2,1)} %bitcast.83) | data formatting | bytes 1253376 | tf_op jit(solution)/shard_map/conv_general_dilated | solution.py:30
  243.1 6.7 %broadcast_select_fusion = f32[128,8,9,32]{3,1,2,0:T(8,128)} fusion(pred[8,9]{0,1:T(8,128)(4,1)S(1)} %copy-done.4, bf16[32,136,1,7,8]{0,3,4,1,2:T(8,128)(2,1)S(1)} %slice.88, bf16[32,136,1,8,9]{0,3,4,1,2:T(8,128)(2,1)S(1)} %copy.38, bf16[3,32,32,3,3]{2,1,4,3,0:T(8,128)(2,1)S(1)} %copy-done.3), kind=kOutput, calls=%fused_computation.25 | convolution fusion | flops 173715456 | bytes 5990400 | tf_op jit(solution)/shard_map/conv_general_dilated | solution.py:30
  249.8 3.8 %copy.39 = f32[128,8,9,32]{0,3,2,1:T(8,128)S(1)} copy(f32[128,8,9,32]{3,1,2,0:T(8,128)} %broadcast_select_fusion) | data formatting | bytes 2359296 | tf_op jit(solution)/shard_map/conv_general_dilated | solution.py:30
  (37 shorter events, 11.3 us)
Async XLA Ops:
  6.5 1.6 copy-start
  6.5 120.6 %all-reduce.2.cloned.1.call-start = ((), (), s32[]{:S(2)}) async-start(), calls=%async_computation | async-start | bytes 262144 | tf_op jit(solution)/shard_map/psum | solution.py:9
  8.1 142.8 %copy-start.1 = (f32[3,32]{1,0:T(4,128)S(1)}, f32[3,32]{1,0:T(4,128)}, u32[]{:S(2)}) copy-start(f32[3,32]{1,0:T(4,128)} %param.10) | copy-start | bytes 1156
  128.7 10.2 %collective-permute-start = (bf16[32,1,64]{1,0,2:T(8,128)(2,1)S(1)}, bf16[32,1,64]{1,0,2:T(8,128)(2,1)S(1)}, u32[]{:S(2)}, u32[]{:S(2)}) collective-permute-start(bf16[32,1,64]{1,0,2:T(8,128)(2,1)S(1)} %get-tuple-element.15), channel_id=1, source_target_pairs={{0,32},{32,64},{64,96},{96,128},{128,160},{160,192},{192,224},{224... | collective-permute-start | bytes 12296 | tf_op jit(solution)/shard_map/ppermute | solution.py:20
  132.8 11.7 %collective-permute-start.1 = (bf16[32,1,64]{1,0,2:T(8,128)(2,1)S(1)}, bf16[32,1,64]{1,0,2:T(8,128)(2,1)S(1)}, u32[]{:S(2)}, u32[]{:S(2)}) collective-permute-start(bf16[32,1,64]{1,0,2:T(8,128)(2,1)S(1)} %get-tuple-element.16), channel_id=1, source_target_pairs={{32,0},{64,32},{96,64},{128,96},{160,128},{192,160},{224,192},{256... | collective-permute-start | bytes 12296 | tf_op jit(solution)/shard_map/ppermute | solution.py:22
  144.6 6.3 %collective-permute-start.2 = (bf16[32,130,1]{1,0,2:T(8,128)(2,1)S(1)}, bf16[32,130,1]{1,0,2:T(8,128)(2,1)S(1)}, u32[]{:S(2)}, u32[]{:S(2)}) collective-permute-start(bf16[32,130,1]{1,0,2:T(8,128)(2,1)S(1)} %get-tuple-element.9), channel_id=1, source_target_pairs={{0,1},{1,2},{2,3},{3,4},{4,5},{5,6},{6,7},{7,8},{8,9},{9,10},{10,1... | collective-permute-start | bytes 24968 | tf_op jit(solution)/shard_map/ppermute | solution.py:20
  149.0 7.8 %collective-permute-start.3 = (bf16[32,130,1]{1,0,2:T(8,128)(2,1)S(1)}, bf16[32,130,1]{1,0,2:T(8,128)(2,1)S(1)}, u32[]{:S(2)}, u32[]{:S(2)}) collective-permute-start(bf16[32,130,1]{1,0,2:T(8,128)(2,1)S(1)} %get-tuple-element.10), channel_id=1, source_target_pairs={{1,0},{2,1},{3,2},{4,3},{5,4},{6,5},{7,6},{8,7},{9,8},{10,9},{11,1... | collective-permute-start | bytes 24968 | tf_op jit(solution)/shard_map/ppermute | solution.py:22
  157.7 4.3 %copy-start.3 = (bf16[3,32,32,3,3]{2,1,4,3,0:T(8,128)(2,1)S(1)}, bf16[3,32,32,3,3]{2,1,4,3,0:T(8,128)(2,1)}, u32[]{:S(2)}) copy-start(bf16[3,32,32,3,3]{2,1,4,3,0:T(8,128)(2,1)} %param.9) | copy-start | bytes 165892
  157.8 4.3 %copy-start.4 = (pred[8,9]{0,1:T(8,128)(4,1)S(1)}, pred[8,9]{0,1:T(8,128)(4,1)}, u32[]{:S(2)}) copy-start(pred[8,9]{0,1:T(8,128)(4,1)} %constant.47) | copy-start | bytes 220
  172.8 9.3 %collective-permute-start.4 = (bf16[32,2,64]{1,0,2:T(8,128)(2,1)S(1)}, bf16[32,2,64]{1,0,2:T(8,128)(2,1)S(1)}, u32[]{:S(2)}, u32[]{:S(2)}) collective-permute-start(bf16[32,2,64]{1,0,2:T(8,128)(2,1)S(1)} %get-tuple-element.13), channel_id=1, source_target_pairs={{0,32},{32,64},{64,96},{96,128},{128,160},{160,192},{192,224},{224... | collective-permute-start | bytes 24584 | tf_op jit(solution)/shard_map/ppermute | solution.py:20
  176.0 11.7 %collective-permute-start.5 = (bf16[32,2,64]{1,0,2:T(8,128)(2,1)S(1)}, bf16[32,2,64]{1,0,2:T(8,128)(2,1)S(1)}, u32[]{:S(2)}, u32[]{:S(2)}) collective-permute-start(bf16[32,2,64]{1,0,2:T(8,128)(2,1)S(1)} %get-tuple-element.14), channel_id=1, source_target_pairs={{32,0},{64,32},{96,64},{128,96},{160,128},{192,160},{224,192},{256... | collective-permute-start | bytes 24584 | tf_op jit(solution)/shard_map/ppermute | solution.py:22
  187.8 5.3 %collective-permute-start.6 = (bf16[32,132,2]{1,0,2:T(8,128)(2,1)S(1)}, bf16[32,132,2]{1,0,2:T(8,128)(2,1)S(1)}, u32[]{:S(2)}, u32[]{:S(2)}) collective-permute-start(bf16[32,132,2]{1,0,2:T(8,128)(2,1)S(1)} %get-tuple-element.7), channel_id=1, source_target_pairs={{0,1},{1,2},{2,3},{3,4},{4,5},{5,6},{6,7},{7,8},{8,9},{9,10},{10,1... | collective-permute-start | bytes 50696 | tf_op jit(solution)/shard_map/ppermute | solution.py:20
  189.7 8.0 %collective-permute-start.7 = (bf16[32,132,2]{1,0,2:T(8,128)(2,1)S(1)}, bf16[32,132,2]{1,0,2:T(8,128)(2,1)S(1)}, u32[]{:S(2)}, u32[]{:S(2)}) collective-permute-start(bf16[32,132,2]{1,0,2:T(8,128)(2,1)S(1)} %get-tuple-element.8), channel_id=1, source_target_pairs={{1,0},{2,1},{3,2},{4,3},{5,4},{6,5},{7,6},{8,7},{9,8},{10,9},{11,1... | collective-permute-start | bytes 50696 | tf_op jit(solution)/shard_map/ppermute | solution.py:22
  212.8 9.0 %collective-permute-start.8 = (bf16[32,4,64]{1,0,2:T(8,128)(2,1)S(1)}, bf16[32,4,64]{1,0,2:T(8,128)(2,1)S(1)}, u32[]{:S(2)}, u32[]{:S(2)}) collective-permute-start(bf16[32,4,64]{1,0,2:T(8,128)(2,1)S(1)} %get-tuple-element.11), channel_id=1, source_target_pairs={{0,32},{32,64},{64,96},{96,128},{128,160},{160,192},{192,224},{224... | collective-permute-start | bytes 49160 | tf_op jit(solution)/shard_map/ppermute | solution.py:20
  215.7 11.7 %collective-permute-start.9 = (bf16[32,4,64]{1,0,2:T(8,128)(2,1)S(1)}, bf16[32,4,64]{1,0,2:T(8,128)(2,1)S(1)}, u32[]{:S(2)}, u32[]{:S(2)}) collective-permute-start(bf16[32,4,64]{1,0,2:T(8,128)(2,1)S(1)} %get-tuple-element.12), channel_id=1, source_target_pairs={{32,0},{64,32},{96,64},{128,96},{160,128},{192,160},{224,192},{256... | collective-permute-start | bytes 49160 | tf_op jit(solution)/shard_map/ppermute | solution.py:22
  227.6 5.5 %collective-permute-start.10 = (bf16[32,136,4]{1,0,2:T(8,128)(2,1)S(1)}, bf16[32,136,4]{1,0,2:T(8,128)(2,1)S(1)}, u32[]{:S(2)}, u32[]{:S(2)}) collective-permute-start(bf16[32,136,4]{1,0,2:T(8,128)(2,1)S(1)} %get-tuple-element.5), channel_id=1, source_target_pairs={{0,1},{1,2},{2,3},{3,4},{4,5},{5,6},{6,7},{7,8},{8,9},{9,10},{10,1... | collective-permute-start | bytes 104456 | tf_op jit(solution)/shard_map/ppermute | solution.py:20
  229.5 8.3 %collective-permute-start.11 = (bf16[32,136,4]{1,0,2:T(8,128)(2,1)S(1)}, bf16[32,136,4]{1,0,2:T(8,128)(2,1)S(1)}, u32[]{:S(2)}, u32[]{:S(2)}) collective-permute-start(bf16[32,136,4]{1,0,2:T(8,128)(2,1)S(1)} %get-tuple-element.6), channel_id=1, source_target_pairs={{1,0},{2,1},{3,2},{4,3},{5,4},{6,5},{7,6},{8,7},{9,8},{10,9},{11,1... | collective-permute-start | bytes 104456 | tf_op jit(solution)/shard_map/ppermute | solution.py:22
  249.8 3.8 %copy-start.2 = (bf16[32]{0:T(256)(128)(2,1)S(1)}, bf16[32]{0:T(256)(128)(2,1)}, u32[]{:S(2)}) copy-start(bf16[32]{0:T(256)(128)(2,1)} %param.11) | copy-start | bytes 196
Sparse Core Ops, SparseCore 0:
  9.6 117.4 all-reduce.1
where the time goes:
time: 262 us; the launch traced here: 261 us
  waiting for transfers between devices  162 us (62%)
  starting transfers between devices  32.9 us (13%)
  local copies, waits for them, and re-layouts  25.1 us (10%)
  matrix products  21.6 us (8%)
  between operations  13.7 us (5%)
  other arithmetic  5.54 us (2%)
    psum x1, waiting for transfers between devices, spread(): return lax.psum(kept, axis)  118 us
    ppermute x6, waiting for transfers between devices, extended(): lax.ppermute(head, axis, [((i + 1) % count, i) for i in range(ends)])  32 us
    conv_general_dilated x9, local copies, waits for them, and re-layouts, dilated_level(): lax.conv_general_dilated(padded[None], weight, (1, 1), 'VALID', rhs_dilat...  22.7 us
    conv_general_dilated x3, matrix products, dilated_level(): lax.conv_general_dilated(padded[None], weight, (1, 1), 'VALID', rhs_dilat...  18.7 us
    ppermute x6, starting transfers between devices, extended(): lax.ppermute(tail, axis, [(i, (i + 1) % count) for i in range(ends)])  18.3 us
    ppermute x6, starting transfers between devices, extended(): lax.ppermute(head, axis, [((i + 1) % count, i) for i in range(ends)])  14.6 us
    ppermute x6, waiting for transfers between devices, extended(): lax.ppermute(tail, axis, [(i, (i + 1) % count) for i in range(ends)])  12.5 us
  transfers between devices with their start and end apart: 13, of which 10 were waited for; matrix products, arithmetic and copies ran while one was open for 0% of the time, Pallas kernels for 0%

commit v1 on v0

--- a/solution.py
+++ b/solution.py
@@ -6,7 +6,7 @@
 
 def spread(value, axis, source):
     kept = jnp.where(lax.axis_index(axis) == source, value, 0).astype(value.dtype)
-    return lax.psum(kept, axis)
+    return jnp.sum(lax.all_gather(kept, axis), axis=0)
 
 
 def extended(cells, sides, width):

time: 262 us -> 188 us (0.72)
  the two profiles are of different devices: /device:TPU:223 before, /device:TPU:31 now
where the time goes in v1:
time: 188 us
  waiting for transfers between devices  89.7 us (48%)
  starting transfers between devices  31.7 us (17%)
  local copies, waits for them, and re-layouts  25.1 us (13%)
  matrix products  20.8 us (11%)
  between operations  13.7 us (7%)
  other arithmetic  6.55 us (3%)
    all_gather x1, waiting for transfers between devices, spread(): return jnp.sum(lax.all_gather(kept, axis), axis=0)  48.8 us
    ppermute x6, waiting for transfers between devices, extended(): lax.ppermute(head, axis, [((i + 1) % count, i) for i in range(ends)])  28.4 us
    conv_general_dilated x9, local copies, waits for them, and re-layouts, dilated_level(): lax.conv_general_dilated(padded[None], weight, (1, 1), 'VALID', rhs_dilat...  22.7 us
    conv_general_dilated x3, matrix products, dilated_level(): lax.conv_general_dilated(padded[None], weight, (1, 1), 'VALID', rhs_dilat...  18.8 us
    ppermute x6, starting transfers between devices, extended(): lax.ppermute(tail, axis, [(i, (i + 1) % count) for i in range(ends)])  17.1 us
    ppermute x6, starting transfers between devices, extended(): lax.ppermute(head, axis, [((i + 1) % count, i) for i in range(ends)])  14.6 us
    ppermute x6, waiting for transfers between devices, extended(): lax.ppermute(tail, axis, [(i, (i + 1) % count) for i in range(ends)])  12.5 us
  transfers between devices with their start and end apart: 13, of which 10 were waited for; matrix products, arithmetic and copies ran while one was open for 1% of the time, Pallas kernels for 0%

profile of v1, /device:TPU:31, one launch (start us, length us, event | category | flops | bytes accessed | tf_op | source)
XLA Modules:
  0.0 187.7 jit_solution(2864178915584927803)
XLA Ops:
  8.3 48.8 %all-gather.3.cloned.1.call-done = bf16[2048,512]{1,0:T(8,128)(2,1)} async-done(((bf16[128,512]{1,0:T(8,128)(2,1)}), bf16[2048,512]{1,0:T(8,128)(2,1)}) %all-gather.3.cloned.1.call-update) | async-done | bytes 2097168 | tf_op jit(solution)/shard_map/all_gather | solution.py:9
  57.1 1.9 %reduce_sum.12 = bf16[128,512]{1,0:T(8,128)(2,1)S(1)} reduce(bf16[16,128,512]{2,1,0:T(8,128)(2,1)} %bitcast.89, bf16[]{:T(256)} %constant.35.clone.1), dimensions={0}, to_apply=%region_0.1 | reduce | flops 983040 | bytes 2228226 | tf_op jit(solution)/shard_map/reduce_sum | solution.py:9
  59.8 2.6 %collective-permute-start = (bf16[32,1,64]{1,0,2:T(8,128)(2,1)S(1)}, bf16[32,1,64]{1,0,2:T(8,128)(2,1)S(1)}, u32[]{:S(2)}, u32[]{:S(2)}) collective-permute-start(bf16[32,1,64]{1,0,2:T(8,128)(2,1)S(1)} %get-tuple-element.15), channel_id=1, source_target_pairs={{0,32},{32,64},{64,96},{96,128},{128,160},{160,192},{192,224},{224... | collective-permute-start | bytes 12296 | tf_op jit(solution)/shard_map/ppermute | solution.py:20
  62.4 1.9 %collective-permute-start.1 = (bf16[32,1,64]{1,0,2:T(8,128)(2,1)S(1)}, bf16[32,1,64]{1,0,2:T(8,128)(2,1)S(1)}, u32[]{:S(2)}, u32[]{:S(2)}) collective-permute-start(bf16[32,1,64]{1,0,2:T(8,128)(2,1)S(1)} %get-tuple-element.16), channel_id=1, source_target_pairs={{32,0},{64,32},{96,64},{128,96},{160,128},{192,160},{224,192},{256... | collective-permute-start | bytes 12296 | tf_op jit(solution)/shard_map/ppermute | solution.py:22
  64.4 4.2 %collective-permute-done = bf16[32,1,64]{1,0,2:T(8,128)(2,1)S(1)} collective-permute-done((bf16[32,1,64]{1,0,2:T(8,128)(2,1)S(1)}, bf16[32,1,64]{1,0,2:T(8,128)(2,1)S(1)}, u32[]{:S(2)}, u32[]{:S(2)}) %collective-permute-start) | collective-permute-done | bytes 4128 | tf_op jit(solution)/shard_map/ppermute | solution.py:20
  68.5 4.4 %collective-permute-done.1 = bf16[32,1,64]{1,0,2:T(8,128)(2,1)S(1)} collective-permute-done((bf16[32,1,64]{1,0,2:T(8,128)(2,1)S(1)}, bf16[32,1,64]{1,0,2:T(8,128)(2,1)S(1)}, u32[]{:S(2)}, u32[]{:S(2)}) %collective-permute-start.1) | collective-permute-done | bytes 4128 | tf_op jit(solution)/shard_map/ppermute | solution.py:22
  73.0 4.3 %collective-permute-start.2 = (bf16[32,130,1]{1,0,2:T(8,128)(2,1)S(1)}, bf16[32,130,1]{1,0,2:T(8,128)(2,1)S(1)}, u32[]{:S(2)}, u32[]{:S(2)}) collective-permute-start(bf16[32,130,1]{1,0,2:T(8,128)(2,1)S(1)} %get-tuple-element.9), channel_id=1, source_target_pairs={{0,1},{1,2},{2,3},{3,4},{4,5},{5,6},{6,7},{7,8},{8,9},{9,10},{10,1... | collective-permute-start | bytes 24968 | tf_op jit(solution)/shard_map/ppermute | solution.py:20
  77.3 1.9 %collective-permute-start.3 = (bf16[32,130,1]{1,0,2:T(8,128)(2,1)S(1)}, bf16[32,130,1]{1,0,2:T(8,128)(2,1)S(1)}, u32[]{:S(2)}, u32[]{:S(2)}) collective-permute-start(bf16[32,130,1]{1,0,2:T(8,128)(2,1)S(1)} %get-tuple-element.10), channel_id=1, source_target_pairs={{1,0},{2,1},{3,2},{4,3},{5,4},{6,5},{7,6},{8,7},{9,8},{10,9},{11,1... | collective-permute-start | bytes 24968 | tf_op jit(solution)/shard_map/ppermute | solution.py:22
  79.3 5.8 %collective-permute-done.3 = bf16[32,130,1]{1,0,2:T(8,128)(2,1)S(1)} collective-permute-done((bf16[32,130,1]{1,0,2:T(8,128)(2,1)S(1)}, bf16[32,130,1]{1,0,2:T(8,128)(2,1)S(1)}, u32[]{:S(2)}, u32[]{:S(2)}) %collective-permute-start.3) | collective-permute-done | bytes 8352 | tf_op jit(solution)/shard_map/ppermute | solution.py:22
  86.1 3.0 %copy.32 = bf16[32,130,1,8,9]{0,3,4,1,2:T(8,128)(2,1)} copy(bf16[32,130,1,8,9]{1,0,4,3,2:T(8,128)(2,1)S(1)} %bitcast.85) | data formatting | bytes 1198080 | tf_op jit(solution)/shard_map/conv_general_dilated | solution.py:30
  90.4 6.6 %broadcast_select_fusion.2 = f32[128,8,9,32]{3,1,2,0:T(8,128)} fusion(pred[8,9]{0,1:T(8,128)(4,1)S(1)} %copy-done.5, bf16[32,130,1,7,2]{0,3,4,1,2:T(8,128)(2,1)S(1)} %slice.80, bf16[32,130,1,8,9]{0,3,4,1,2:T(8,128)(2,1)} %copy.32, bf16[3,32,32,3,3]{2,1,4,3,0:T(8,128)(2,1)S(1)} %copy-done.4), kind=kOutput, calls=%fused_computation.27 | convolution fusion | flops 172360704 | bytes 2386944 | tf_op jit(solution)/shard_map/conv_general_dilated | solution.py:30
  97.0 3.7 %copy.33 = f32[128,8,9,32]{0,3,2,1:T(8,128)S(1)} copy(f32[128,8,9,32]{3,1,2,0:T(8,128)} %broadcast_select_fusion.2) | data formatting | bytes 2359296 | tf_op jit(solution)/shard_map/conv_general_dilated | solution.py:30
  101.1 3.2 %collective-permute-start.4 = (bf16[32,2,64]{1,0,2:T(8,128)(2,1)S(1)}, bf16[32,2,64]{1,0,2:T(8,128)(2,1)S(1)}, u32[]{:S(2)}, u32[]{:S(2)}) collective-permute-start(bf16[32,2,64]{1,0,2:T(8,128)(2,1)S(1)} %get-tuple-element.13), channel_id=1, source_target_pairs={{0,32},{32,64},{64,96},{96,128},{128,160},{160,192},{192,224},{224... | collective-permute-start | bytes 24584 | tf_op jit(solution)/shard_map/ppermute | solution.py:20
  104.3 1.9 %collective-permute-start.5 = (bf16[32,2,64]{1,0,2:T(8,128)(2,1)S(1)}, bf16[32,2,64]{1,0,2:T(8,128)(2,1)S(1)}, u32[]{:S(2)}, u32[]{:S(2)}) collective-permute-start(bf16[32,2,64]{1,0,2:T(8,128)(2,1)S(1)} %get-tuple-element.14), channel_id=1, source_target_pairs={{32,0},{64,32},{96,64},{128,96},{160,128},{192,160},{224,192},{256... | collective-permute-start | bytes 24584 | tf_op jit(solution)/shard_map/ppermute | solution.py:22
  106.3 4.2 %collective-permute-done.4 = bf16[32,2,64]{1,0,2:T(8,128)(2,1)S(1)} collective-permute-done((bf16[32,2,64]{1,0,2:T(8,128)(2,1)S(1)}, bf16[32,2,64]{1,0,2:T(8,128)(2,1)S(1)}, u32[]{:S(2)}, u32[]{:S(2)}) %collective-permute-start.4) | collective-permute-done | bytes 8224 | tf_op jit(solution)/shard_map/ppermute | solution.py:20
  110.4 4.4 %collective-permute-done.5 = bf16[32,2,64]{1,0,2:T(8,128)(2,1)S(1)} collective-permute-done((bf16[32,2,64]{1,0,2:T(8,128)(2,1)S(1)}, bf16[32,2,64]{1,0,2:T(8,128)(2,1)S(1)}, u32[]{:S(2)}, u32[]{:S(2)}) %collective-permute-start.5) | collective-permute-done | bytes 8224 | tf_op jit(solution)/shard_map/ppermute | solution.py:22
  114.9 1.9 %collective-permute-start.6 = (bf16[32,132,2]{1,0,2:T(8,128)(2,1)S(1)}, bf16[32,132,2]{1,0,2:T(8,128)(2,1)S(1)}, u32[]{:S(2)}, u32[]{:S(2)}) collective-permute-start(bf16[32,132,2]{1,0,2:T(8,128)(2,1)S(1)} %get-tuple-element.7), channel_id=1, source_target_pairs={{0,1},{1,2},{2,3},{3,4},{4,5},{5,6},{6,7},{7,8},{8,9},{9,10},{10,1... | collective-permute-start | bytes 50696 | tf_op jit(solution)/shard_map/ppermute | solution.py:20
  116.9 3.4 %collective-permute-start.7 = (bf16[32,132,2]{1,0,2:T(8,128)(2,1)S(1)}, bf16[32,132,2]{1,0,2:T(8,128)(2,1)S(1)}, u32[]{:S(2)}, u32[]{:S(2)}) collective-permute-start(bf16[32,132,2]{1,0,2:T(8,128)(2,1)S(1)} %get-tuple-element.8), channel_id=1, source_target_pairs={{1,0},{2,1},{3,2},{4,3},{5,4},{6,5},{7,6},{8,7},{9,8},{10,9},{11,1... | collective-permute-start | bytes 50696 | tf_op jit(solution)/shard_map/ppermute | solution.py:22
  120.2 4.6 %collective-permute-done.7 = bf16[32,132,2]{1,0,2:T(8,128)(2,1)S(1)} collective-permute-done((bf16[32,132,2]{1,0,2:T(8,128)(2,1)S(1)}, bf16[32,132,2]{1,0,2:T(8,128)(2,1)S(1)}, u32[]{:S(2)}, u32[]{:S(2)}) %collective-permute-start.7) | collective-permute-done | bytes 16928 | tf_op jit(solution)/shard_map/ppermute | solution.py:22
  126.8 3.3 %copy.35 = bf16[32,132,1,8,9]{0,3,4,1,2:T(8,128)(2,1)S(1)} copy(bf16[32,132,1,8,9]{1,0,4,3,2:T(8,128)(2,1)} %bitcast.83) | data formatting | bytes 1216512 | tf_op jit(solution)/shard_map/conv_general_dilated | solution.py:30
  130.4 5.5 %broadcast_select_fusion.1 = f32[128,8,9,32]{3,1,2,0:T(8,128)} fusion(pred[8,9]{0,1:T(8,128)(4,1)S(1)} %copy-done.5, bf16[32,132,1,7,4]{0,3,4,1,2:T(8,128)(2,1)S(1)} %slice.84, bf16[32,132,1,8,9]{0,3,4,1,2:T(8,128)(2,1)S(1)} %copy.35, bf16[3,32,32,3,3]{2,1,4,3,0:T(8,128)(2,1)S(1)} %copy-done.4), kind=kOutput, calls=%fused_computation.26 | convolution fusion | flops 172800000 | bytes 4769792 | tf_op jit(solution)/shard_map/conv_general_dilated | solution.py:30
  135.9 3.7 %copy.36 = f32[128,8,9,32]{0,3,2,1:T(8,128)S(1)} copy(f32[128,8,9,32]{3,1,2,0:T(8,128)} %broadcast_select_fusion.1) | data formatting | bytes 2359296 | tf_op jit(solution)/shard_map/conv_general_dilated | solution.py:30
  140.0 3.2 %collective-permute-start.8 = (bf16[32,4,64]{1,0,2:T(8,128)(2,1)S(1)}, bf16[32,4,64]{1,0,2:T(8,128)(2,1)S(1)}, u32[]{:S(2)}, u32[]{:S(2)}) collective-permute-start(bf16[32,4,64]{1,0,2:T(8,128)(2,1)S(1)} %get-tuple-element.11), channel_id=1, source_target_pairs={{0,32},{32,64},{64,96},{96,128},{128,160},{160,192},{192,224},{224... | collective-permute-start | bytes 49160 | tf_op jit(solution)/shard_map/ppermute | solution.py:20
  143.2 1.9 %collective-permute-start.9 = (bf16[32,4,64]{1,0,2:T(8,128)(2,1)S(1)}, bf16[32,4,64]{1,0,2:T(8,128)(2,1)S(1)}, u32[]{:S(2)}, u32[]{:S(2)}) collective-permute-start(bf16[32,4,64]{1,0,2:T(8,128)(2,1)S(1)} %get-tuple-element.12), channel_id=1, source_target_pairs={{32,0},{64,32},{96,64},{128,96},{160,128},{192,160},{224,192},{256... | collective-permute-start | bytes 49160 | tf_op jit(solution)/shard_map/ppermute | solution.py:22
  145.2 4.2 %collective-permute-done.8 = bf16[32,4,64]{1,0,2:T(8,128)(2,1)S(1)} collective-permute-done((bf16[32,4,64]{1,0,2:T(8,128)(2,1)S(1)}, bf16[32,4,64]{1,0,2:T(8,128)(2,1)S(1)}, u32[]{:S(2)}, u32[]{:S(2)}) %collective-permute-start.8) | collective-permute-done | bytes 16416 | tf_op jit(solution)/shard_map/ppermute | solution.py:20
  149.3 4.4 %collective-permute-done.9 = bf16[32,4,64]{1,0,2:T(8,128)(2,1)S(1)} collective-permute-done((bf16[32,4,64]{1,0,2:T(8,128)(2,1)S(1)}, bf16[32,4,64]{1,0,2:T(8,128)(2,1)S(1)}, u32[]{:S(2)}, u32[]{:S(2)}) %collective-permute-start.9) | collective-permute-done | bytes 16416 | tf_op jit(solution)/shard_map/ppermute | solution.py:22
  153.9 1.9 %collective-permute-start.10 = (bf16[32,136,4]{1,0,2:T(8,128)(2,1)S(1)}, bf16[32,136,4]{1,0,2:T(8,128)(2,1)S(1)}, u32[]{:S(2)}, u32[]{:S(2)}) collective-permute-start(bf16[32,136,4]{1,0,2:T(8,128)(2,1)S(1)} %get-tuple-element.5), channel_id=1, source_target_pairs={{0,1},{1,2},{2,3},{3,4},{4,5},{5,6},{6,7},{7,8},{8,9},{9,10},{10,1... | collective-permute-start | bytes 104456 | tf_op jit(solution)/shard_map/ppermute | solution.py:20
  155.8 3.5 %collective-permute-start.11 = (bf16[32,136,4]{1,0,2:T(8,128)(2,1)S(1)}, bf16[32,136,4]{1,0,2:T(8,128)(2,1)S(1)}, u32[]{:S(2)}, u32[]{:S(2)}) collective-permute-start(bf16[32,136,4]{1,0,2:T(8,128)(2,1)S(1)} %get-tuple-element.6), channel_id=1, source_target_pairs={{1,0},{2,1},{3,2},{4,3},{5,4},{6,5},{7,6},{8,7},{9,8},{10,9},{11,1... | collective-permute-start | bytes 104456 | tf_op jit(solution)/shard_map/ppermute | solution.py:22
  159.4 4.8 %collective-permute-done.11 = bf16[32,136,4]{1,0,2:T(8,128)(2,1)S(1)} collective-permute-done((bf16[32,136,4]{1,0,2:T(8,128)(2,1)S(1)}, bf16[32,136,4]{1,0,2:T(8,128)(2,1)S(1)}, u32[]{:S(2)}, u32[]{:S(2)}) %collective-permute-start.11) | collective-permute-done | bytes 34848 | tf_op jit(solution)/shard_map/ppermute | solution.py:22
  165.8 3.0 %copy.38 = bf16[32,136,1,8,9]{0,3,4,1,2:T(8,128)(2,1)S(1)} copy(bf16[32,136,1,8,9]{1,0,4,3,2:T(8,128)(2,1)} %bitcast.84) | data formatting | bytes 1253376 | tf_op jit(solution)/shard_map/conv_general_dilated | solution.py:30
  169.4 6.7 %broadcast_select_fusion = f32[128,8,9,32]{3,1,2,0:T(8,128)} fusion(pred[8,9]{0,1:T(8,128)(4,1)S(1)} %copy-done.5, bf16[32,136,1,7,8]{0,3,4,1,2:T(8,128)(2,1)S(1)} %slice.88, bf16[32,136,1,8,9]{0,3,4,1,2:T(8,128)(2,1)S(1)} %copy.38, bf16[3,32,32,3,3]{2,1,4,3,0:T(8,128)(2,1)S(1)} %copy-done.4), kind=kOutput, calls=%fused_computation.25 | convolution fusion | flops 173715456 | bytes 5990400 | tf_op jit(solution)/shard_map/conv_general_dilated | solution.py:30
  176.1 3.8 %copy.39 = f32[128,8,9,32]{0,3,2,1:T(8,128)S(1)} copy(f32[128,8,9,32]{3,1,2,0:T(8,128)} %broadcast_select_fusion) | data formatting | bytes 2359296 | tf_op jit(solution)/shard_map/conv_general_dilated | solution.py:30
  (40 shorter events, 11.3 us)
Async XLA Ops:
  6.5 0.8 copy-start
  6.5 52.5 %copy-start.1 = (bf16[512,32]{0,1:T(8,128)(2,1)S(1)}, bf16[512,32]{0,1:T(8,128)(2,1)}, u32[]{:S(2)}) copy-start(bf16[512,32]{0,1:T(8,128)(2,1)} %param.8) | copy-start | bytes 98308
  6.5 50.6 %all-gather.3.cloned.1.call-start = ((), (), s32[]{:S(2)}) async-start(), calls=%async_computation | async-start | bytes 2228224 | tf_op jit(solution)/shard_map/all_gather | solution.py:9
  59.0 20.3 %copy-start.2 = (f32[3,32]{1,0:T(4,128)S(1)}, f32[3,32]{1,0:T(4,128)}, u32[]{:S(2)}) copy-start(f32[3,32]{1,0:T(4,128)} %param.10) | copy-start | bytes 1156
  59.8 8.7 %collective-permute-start = (bf16[32,1,64]{1,0,2:T(8,128)(2,1)S(1)}, bf16[32,1,64]{1,0,2:T(8,128)(2,1)S(1)}, u32[]{:S(2)}, u32[]{:S(2)}) collective-permute-start(bf16[32,1,64]{1,0,2:T(8,128)(2,1)S(1)} %get-tuple-element.15), channel_id=1, source_target_pairs={{0,32},{32,64},{64,96},{96,128},{128,160},{160,192},{192,224},{224... | collective-permute-start | bytes 12296 | tf_op jit(solution)/shard_map/ppermute | solution.py:20
  62.4 10.5 %collective-permute-start.1 = (bf16[32,1,64]{1,0,2:T(8,128)(2,1)S(1)}, bf16[32,1,64]{1,0,2:T(8,128)(2,1)S(1)}, u32[]{:S(2)}, u32[]{:S(2)}) collective-permute-start(bf16[32,1,64]{1,0,2:T(8,128)(2,1)S(1)} %get-tuple-element.16), channel_id=1, source_target_pairs={{32,0},{64,32},{96,64},{128,96},{160,128},{192,160},{224,192},{256... | collective-permute-start | bytes 12296 | tf_op jit(solution)/shard_map/ppermute | solution.py:22
  73.0 6.3 %collective-permute-start.2 = (bf16[32,130,1]{1,0,2:T(8,128)(2,1)S(1)}, bf16[32,130,1]{1,0,2:T(8,128)(2,1)S(1)}, u32[]{:S(2)}, u32[]{:S(2)}) collective-permute-start(bf16[32,130,1]{1,0,2:T(8,128)(2,1)S(1)} %get-tuple-element.9), channel_id=1, source_target_pairs={{0,1},{1,2},{2,3},{3,4},{4,5},{5,6},{6,7},{7,8},{8,9},{9,10},{10,1... | collective-permute-start | bytes 24968 | tf_op jit(solution)/shard_map/ppermute | solution.py:20
  77.3 7.8 %collective-permute-start.3 = (bf16[32,130,1]{1,0,2:T(8,128)(2,1)S(1)}, bf16[32,130,1]{1,0,2:T(8,128)(2,1)S(1)}, u32[]{:S(2)}, u32[]{:S(2)}) collective-permute-start(bf16[32,130,1]{1,0,2:T(8,128)(2,1)S(1)} %get-tuple-element.10), channel_id=1, source_target_pairs={{1,0},{2,1},{3,2},{4,3},{5,4},{6,5},{7,6},{8,7},{9,8},{10,9},{11,1... | collective-permute-start | bytes 24968 | tf_op jit(solution)/shard_map/ppermute | solution.py:22
  86.1 4.3 %copy-start.4 = (bf16[3,32,32,3,3]{2,1,4,3,0:T(8,128)(2,1)S(1)}, bf16[3,32,32,3,3]{2,1,4,3,0:T(8,128)(2,1)}, u32[]{:S(2)}) copy-start(bf16[3,32,32,3,3]{2,1,4,3,0:T(8,128)(2,1)} %param.9) | copy-start | bytes 165892
  86.1 4.3 %copy-start.5 = (pred[8,9]{0,1:T(8,128)(4,1)S(1)}, pred[8,9]{0,1:T(8,128)(4,1)}, u32[]{:S(2)}) copy-start(pred[8,9]{0,1:T(8,128)(4,1)} %constant.49) | copy-start | bytes 220
  101.1 9.3 %collective-permute-start.4 = (bf16[32,2,64]{1,0,2:T(8,128)(2,1)S(1)}, bf16[32,2,64]{1,0,2:T(8,128)(2,1)S(1)}, u32[]{:S(2)}, u32[]{:S(2)}) collective-permute-start(bf16[32,2,64]{1,0,2:T(8,128)(2,1)S(1)} %get-tuple-element.13), channel_id=1, source_target_pairs={{0,32},{32,64},{64,96},{96,128},{128,160},{160,192},{192,224},{224... | collective-permute-start | bytes 24584 | tf_op jit(solution)/shard_map/ppermute | solution.py:20
  104.3 10.5 %collective-permute-start.5 = (bf16[32,2,64]{1,0,2:T(8,128)(2,1)S(1)}, bf16[32,2,64]{1,0,2:T(8,128)(2,1)S(1)}, u32[]{:S(2)}, u32[]{:S(2)}) collective-permute-start(bf16[32,2,64]{1,0,2:T(8,128)(2,1)S(1)} %get-tuple-element.14), channel_id=1, source_target_pairs={{32,0},{64,32},{96,64},{128,96},{160,128},{192,160},{224,192},{256... | collective-permute-start | bytes 24584 | tf_op jit(solution)/shard_map/ppermute | solution.py:22
  114.9 5.3 %collective-permute-start.6 = (bf16[32,132,2]{1,0,2:T(8,128)(2,1)S(1)}, bf16[32,132,2]{1,0,2:T(8,128)(2,1)S(1)}, u32[]{:S(2)}, u32[]{:S(2)}) collective-permute-start(bf16[32,132,2]{1,0,2:T(8,128)(2,1)S(1)} %get-tuple-element.7), channel_id=1, source_target_pairs={{0,1},{1,2},{2,3},{3,4},{4,5},{5,6},{6,7},{7,8},{8,9},{9,10},{10,1... | collective-permute-start | bytes 50696 | tf_op jit(solution)/shard_map/ppermute | solution.py:20
  116.9 8.0 %collective-permute-start.7 = (bf16[32,132,2]{1,0,2:T(8,128)(2,1)S(1)}, bf16[32,132,2]{1,0,2:T(8,128)(2,1)S(1)}, u32[]{:S(2)}, u32[]{:S(2)}) collective-permute-start(bf16[32,132,2]{1,0,2:T(8,128)(2,1)S(1)} %get-tuple-element.8), channel_id=1, source_target_pairs={{1,0},{2,1},{3,2},{4,3},{5,4},{6,5},{7,6},{8,7},{9,8},{10,9},{11,1... | collective-permute-start | bytes 50696 | tf_op jit(solution)/shard_map/ppermute | solution.py:22
  140.0 9.3 %collective-permute-start.8 = (bf16[32,4,64]{1,0,2:T(8,128)(2,1)S(1)}, bf16[32,4,64]{1,0,2:T(8,128)(2,1)S(1)}, u32[]{:S(2)}, u32[]{:S(2)}) collective-permute-start(bf16[32,4,64]{1,0,2:T(8,128)(2,1)S(1)} %get-tuple-element.11), channel_id=1, source_target_pairs={{0,32},{32,64},{64,96},{96,128},{128,160},{160,192},{192,224},{224... | collective-permute-start | bytes 49160 | tf_op jit(solution)/shard_map/ppermute | solution.py:20
  143.2 10.5 %collective-permute-start.9 = (bf16[32,4,64]{1,0,2:T(8,128)(2,1)S(1)}, bf16[32,4,64]{1,0,2:T(8,128)(2,1)S(1)}, u32[]{:S(2)}, u32[]{:S(2)}) collective-permute-start(bf16[32,4,64]{1,0,2:T(8,128)(2,1)S(1)} %get-tuple-element.12), channel_id=1, source_target_pairs={{32,0},{64,32},{96,64},{128,96},{160,128},{192,160},{224,192},{256... | collective-permute-start | bytes 49160 | tf_op jit(solution)/shard_map/ppermute | solution.py:22
  153.9 5.5 %collective-permute-start.10 = (bf16[32,136,4]{1,0,2:T(8,128)(2,1)S(1)}, bf16[32,136,4]{1,0,2:T(8,128)(2,1)S(1)}, u32[]{:S(2)}, u32[]{:S(2)}) collective-permute-start(bf16[32,136,4]{1,0,2:T(8,128)(2,1)S(1)} %get-tuple-element.5), channel_id=1, source_target_pairs={{0,1},{1,2},{2,3},{3,4},{4,5},{5,6},{6,7},{7,8},{8,9},{9,10},{10,1... | collective-permute-start | bytes 104456 | tf_op jit(solution)/shard_map/ppermute | solution.py:20
  155.8 8.3 %collective-permute-start.11 = (bf16[32,136,4]{1,0,2:T(8,128)(2,1)S(1)}, bf16[32,136,4]{1,0,2:T(8,128)(2,1)S(1)}, u32[]{:S(2)}, u32[]{:S(2)}) collective-permute-start(bf16[32,136,4]{1,0,2:T(8,128)(2,1)S(1)} %get-tuple-element.6), channel_id=1, source_target_pairs={{1,0},{2,1},{3,2},{4,3},{5,4},{6,5},{7,6},{8,7},{9,8},{10,9},{11,1... | collective-permute-start | bytes 104456 | tf_op jit(solution)/shard_map/ppermute | solution.py:22
  176.1 3.8 %copy-start.3 = (bf16[32]{0:T(256)(128)(2,1)S(1)}, bf16[32]{0:T(256)(128)(2,1)}, u32[]{:S(2)}) copy-start(bf16[32]{0:T(256)(128)(2,1)} %param.11) | copy-start | bytes 196
Sparse Core Ops, SparseCore 0:
  9.5 47.5 all-gather.2
